TPU v7x, 32 devices: a whole 2x2x4 slice. The times are simulated.
32 devices in a mesh: row: 2 (over x), col: 16 (over z, y, core).
Axes of the slice: x: 2, y: 2, z: 4, core: 2. Of those that a mesh axis runs over, the one named last changes fastest.
Arguments:
- activations: bfloat16 [128, 8192], P('col', 'row'), may hold values from -6 to 6
- up_weight: bfloat16 [8192, 53248], P('row', 'col'), may hold values from -0.0625 to 0.0625
- out_grad: bfloat16 [128, 53248], P('row', 'col'), may hold values from -6 to 6
- round_seed: int32 [1], replicated, may hold values from 0 to 1073741823
- counter_base: int32 [128], P('row'), may hold values from 0 to 1073741823
Outputs:
- weight_grad: float32 [8192, 53248], P('row', 'col')
- input_grad: bfloat16 [128, 8192], P('col', 'row')
All inputs are finite; a program needn't handle non-finite values.
Results may differ from a plain program's by a relative error of at most 0.015.
Values may be sent and summed in bfloat16 or wider, within the bound.
No kernel may reach another device: no remote copies, remote signals or barrier semaphores. Data moves between devices by JAX's collectives and lax.ppermute only.
A program may use at most 192 MiB of HBM per device.

v0:
```python
import jax
import jax.numpy as jnp
from jax import lax
from jax.sharding import PartitionSpec as P


def stochastic_round(grad, counter_base, round_seed, col_first):
    columns = col_first + lax.broadcasted_iota(jnp.int32, grad.shape, 1)
    counter = counter_base[:, None] + columns
    mixed = counter * jnp.int32(747796405) + round_seed[0] * jnp.int32(1013904223)
    mixed = mixed ^ mixed >> 15
    mixed = mixed * jnp.int32(277803737)
    mixed = mixed ^ mixed >> 16
    level = (mixed & 255).astype(jnp.float32)
    scaled = grad.astype(jnp.float32) * 4.0 + (level + 0.5) / 256.0
    return (jnp.floor(scaled) / 4.0).astype(jnp.bfloat16)


def contract(left, right):
    return lax.dot_general(
        left, right, (((0,), (0,)), ((), ())), preferred_element_type=jnp.float32
    )


def project(grad_rows, weight):
    return lax.dot_general(
        grad_rows, weight, (((1,), (1,)), ((), ())), preferred_element_type=jnp.float32
    )


def fold_panels(activations, combine, initial):
    everyone = lax.all_gather(activations, "col", axis=0, tiled=True)
    return combine(initial, everyone, 0)


def shards(activations, up_weight, out_grad, round_seed, counter_base):
    ff_local = out_grad.shape[1]
    d_local = activations.shape[1]
    col_first = lax.axis_index("col") * ff_local
    quantized = stochastic_round(out_grad, counter_base, round_seed, col_first)
    total_tokens = activations.shape[0] * lax.axis_size("col")
    scaling = total_tokens ** (-0.5)
    grad_zero = jnp.zeros((d_local, ff_local), jnp.float32)
    everything = lax.all_gather(quantized, "row", axis=0, tiled=True)

    def accumulate(total, panel, offset):
        return contract(panel, everything)

    weight_grad = fold_panels(activations, accumulate, grad_zero)
    input_grad = lax.psum_scatter(
        project(everything, up_weight).astype(jnp.bfloat16), "col", scatter_dimension=0, tiled=True
    )
    return (weight_grad * scaling, input_grad)


def solution(mesh):
    placed = (P("col", "row"), P("row", "col"), P("row", "col"), P(), P("row"))
    return jax.shard_map(
        shards,
        mesh=mesh,
        in_specs=placed,
        out_specs=(P("row", "col"), P("col", "row")),
        check_vma=False,
    )
```

profile of v0, /device:TPU:0, one launch (start us, length us, event | category | flops | bytes accessed | tf_op | source)
XLA Modules:
  0.0 130.5 jit_solution(6275972824914543225)
XLA Ops:
  7.2 0.0 all-gather.2.cloned.1.call-start
  7.2 0.7 all-gather.2.cloned.1.call-update
  7.9 0.0 reduce-scatter.2.cloned.1.call-start
  8.6 1.6 %fusion.8 = bf16[64,3328]{1,0:T(8,128)(2,1)S(1)} fusion(bf16[64,3328]{1,0:T(8,128)(2,1)} %param.7, s32[]{:T(128)} %bitcast, s32[3328]{0:T(1024)S(1)} %iota_add_fusion, s32[64]{0:T(128)} %param.9), kind=kLoop, calls=%fused_computation.12 | loop fusion | flops 3833856 | bytes 865540 | tf_op jit(solution)/shard_map/convert_element_type | solution.py:16
  10.2 13.5 %all_gather.6 = bf16[128,3328]{1,0:T(8,128)(2,1)S(1)} all-gather(bf16[64,3328]{1,0:T(8,128)(2,1)S(1)} %fusion.8), channel_id=1, replica_groups=mesh['row'=2,'col'=16] {'row'}, dimensions={0}, use_global_device_ids=true | all-gather | bytes 1277952 | tf_op jit(solution)/shard_map/all_gather | solution.py:44
  23.6 15.0 %convolution_convert_fusion = bf16[128,4096]{1,0:T(8,128)(2,1)} fusion(bf16[128,3328]{1,0:T(8,128)(2,1)S(1)} %all_gather.6, bf16[4096,3328]{1,0:T(8,128)(2,1)} %param.6), kind=kOutput, calls=%fused_computation.1 | convolution fusion | flops 3490185216 | bytes 29163520 | tf_op jit(solution)/shard_map/dot_general | solution.py:26
  38.6 0.0 reduce-scatter.2.cloned.1.call-update
  38.7 12.1 %all-gather.2.cloned.1.call-done = bf16[128,4096]{1,0:T(8,128)(2,1)} async-done(((bf16[8,4096]{1,0:T(8,128)(2,1)}), bf16[128,4096]{1,0:T(8,128)(2,1)}) %all-gather.2.cloned.1.call-update) | async-done | bytes 1048592 | tf_op jit(solution)/shard_map/all_gather | solution.py:32
  50.8 22.8 %multiply_bitcast_fusion = f32[4096,3328]{0,1:T(8,128)} fusion(bf16[128,3328]{1,0:T(8,128)(2,1)S(1)} %all_gather.6, bf16[128,4096]{1,0:T(8,128)(2,1)} %all-gather.2.cloned.1.call-done), kind=kOutput, calls=%fused_computation | convolution fusion | flops 3503292416 | bytes 56426496 | tf_op jit(solution)/shard_map/dot_general | solution.py:20
  73.6 50.1 %copy.7 = f32[4096,3328]{1,0:T(8,128)} copy(f32[4096,3328]{0,1:T(8,128)} %multiply_bitcast_fusion) | data formatting | bytes 109051904
  123.7 0.0 reduce-scatter.2.cloned.1.call-done
  (1 shorter events, 0.0 us)
Async XLA Ops:
  7.2 43.6 %all-gather.2.cloned.1.call-start = ((), (), s32[]{:S(2)}) async-start(), calls=%async_computation.1 | async-start | bytes 1114112 | tf_op jit(solution)/shard_map/all_gather | solution.py:32
  7.9 115.8 %reduce-scatter.2.cloned.1.call-start = ((), (), s32[]{:S(2)}) async-start(), calls=%async_computation.2 | async-start | bytes 1114112 | tf_op jit(solution)/shard_map/reduce_scatter | solution.py:50
Sparse Core Ops, SparseCore 0:
  10.1 40.5 all-gather.1
  54.9 56.5 reduce-scatter.1
where the time goes:
time: 131 us
  local copies, waits for them, and re-layouts  50.1 us (38%)
  matrix products  37.8 us (29%)
  between operations  14.7 us (11%)
  blocking collectives  13.5 us (10%)
  waiting for transfers between devices  12.8 us (10%)
  other arithmetic  1.56 us (1%)
    unnamed x1, local copies, waits for them, and re-layouts  50.1 us
    dot_general x1, matrix products, contract(): lax.dot_general(left, right, (((0,), (0,)), ((), ())), preferred_element_...  22.8 us
    dot_general x1, matrix products, project(): lax.dot_general(grad_rows, weight, (((1,), (1,)), ((), ())), preferred_el...  15 us
    all_gather x1, blocking collectives, shards(): everything = lax.all_gather(quantized, 'row', axis=0, tiled=True)  13.5 us
    all_gather x1, waiting for transfers between devices, fold_panels(): everyone = lax.all_gather(activations, 'col', axis=0, tiled=True)  12.1 us
  transfers between devices with their start and end apart: 2, of which 1 were waited for; matrix products, arithmetic and copies ran while one was open for 69% of the time, Pallas kernels for 0%

commit v1 on v0

v1 whole, which is shorter than its diff:
```python
import functools

import jax
import jax.numpy as jnp
from jax import lax
from jax.experimental import pallas as pl
from jax.experimental.pallas import tpu as pltpu
from jax.sharding import PartitionSpec as P


CORES = 2
MIB = 2**20


def round_kernel(per_col, seed_ref, base_ref, grad_ref, out_ref):
    rows, f_local = grad_ref.shape
    shape = (rows, rows)
    diagonal = lax.broadcasted_iota(jnp.int32, shape, 0) == lax.broadcasted_iota(
        jnp.int32, shape, 1
    )
    base = jnp.where(diagonal, jnp.broadcast_to(base_ref[...], shape), 0)
    base = jnp.sum(base, axis=1, keepdims=True)
    col_first = lax.axis_index("col") * f_local
    offset = seed_ref[0] * jnp.int32(1013904223)
    width = largest_block(f_local, 256)
    for start in range(0, f_local, width):
        columns = lax.broadcasted_iota(jnp.int32, (rows, width), 1) + (col_first + start)
        mixed = (base + columns) * jnp.int32(747796405) + offset
        mixed = mixed ^ (mixed >> 15)
        mixed = mixed * jnp.int32(277803737)
        mixed = mixed ^ (mixed >> 16)
        level = (mixed & 255).astype(jnp.float32)
        grad = grad_ref[:, start : start + width].astype(jnp.float32)
        done = jnp.floor(grad * 4.0 + (level + 0.5) / 256.0) / 4.0
        pieces = [done[i : i + per_col] for i in range(0, rows, per_col)]
        pieces = [p for c in range(CORES) for p in pieces[c::CORES]]
        out_ref[:, start : start + width] = jnp.concatenate(pieces).astype(out_ref.dtype)


def stochastic_round(grad, counter_base, round_seed, per_col):
    vmem = pl.BlockSpec(memory_space=pltpu.VMEM)
    return pl.pallas_call(
        functools.partial(round_kernel, per_col),
        out_shape=jax.ShapeDtypeStruct(grad.shape, jnp.bfloat16),
        in_specs=[pl.BlockSpec(memory_space=pltpu.SMEM), vmem, vmem],
        out_specs=vmem,
        name="quantize",
        cost_estimate=pl.CostEstimate(
            flops=16 * grad.size, bytes_accessed=4 * grad.size, transcendentals=0
        ),
        compiler_params=pltpu.CompilerParams(vmem_limit_bytes=8 * MIB),
    )(round_seed, counter_base[None, :], grad)


def largest_block(length, most):
    return next(b for b in range(min(most, length), 0, -1) if length % b == 0)


def row_start(j, rows, size):
    owner = lax.rem(lax.axis_index("row") - j + rows, rows)
    return pl.multiple_of(owner * size, size)


def project_kernel(n_row, block, *refs):
    q_refs, (w_hbm, keep_ref, give_ref, w_ref, sems) = refs[:n_row], refs[n_row:]
    tr = q_refs[0].shape[0]
    half = tr // CORES
    core = lax.rem(lax.axis_index("col"), CORES)

    def fetch(step):
        ds = pl.ds(pl.multiple_of(step * block, block), block)
        return pltpu.make_async_copy(w_hbm.at[ds, :], w_ref.at[ds, :], sems.at[step])

    steps = w_ref.shape[0] // block
    for step in range(steps):
        fetch(step).start()

    @pl.loop(0, steps)
    def _(step):
        fetch(step).wait()
        ds = pl.ds(pl.multiple_of(step * block, block), block)
        q = jnp.concatenate([q_ref[...] for q_ref in q_refs], axis=0)
        whole = lax.dot_general(
            w_ref[ds, :], q, (((1,), (1,)), ((), ())), preferred_element_type=jnp.float32
        )
        whole = whole.T.astype(jnp.bfloat16)
        for c in range(CORES):

            @pl.when(core == c)
            def _():
                for j in range(n_row):
                    at = pl.ds(row_start(j, n_row, half), half)
                    for k in range(CORES):
                        piece = whole[j * tr + k * half : j * tr + (k + 1) * half]
                        (keep_ref if k == c else give_ref)[at, ds] = piece


def project(q_parts, up_weight):
    n_row = len(q_parts)
    tokens = q_parts[0].shape[0] * n_row
    d_local, f_local = up_weight.shape
    block = largest_block(d_local, 512)
    vmem = pl.BlockSpec(memory_space=pltpu.VMEM)
    return pl.pallas_call(
        functools.partial(project_kernel, n_row, block),
        out_shape=[jax.ShapeDtypeStruct((tokens // CORES, d_local), jnp.bfloat16)] * 2,
        in_specs=[vmem] * n_row + [pl.BlockSpec(memory_space=pl.ANY)],
        out_specs=[vmem] * 2,
        scratch_shapes=[
            pltpu.VMEM(up_weight.shape, up_weight.dtype),
            pltpu.SemaphoreType.DMA((d_local // block,)),
        ],
        name="project",
        cost_estimate=pl.CostEstimate(
            flops=2 * tokens * d_local * f_local,
            bytes_accessed=2 * d_local * f_local,
            transcendentals=0,
        ),
        compiler_params=pltpu.CompilerParams(vmem_limit_bytes=VMEM_PROJECT * MIB),
    )(*q_parts, up_weight)


VMEM_PROJECT = 44
VMEM_WGRAD = 32


def wgrad_kernel(n_row, scaling, *refs):
    q_refs, (mine_ref, other_ref, out_ref, x_ref) = refs[:n_row], refs[n_row:]
    tr = q_refs[0].shape[0]
    half = tr // CORES
    block = out_ref.shape[0]
    core = lax.rem(lax.axis_index("col"), CORES)
    for c in range(CORES):

        @pl.when((pl.program_id(0) == 0) & (core == c))
        def _():
            for j in range(n_row):
                at = pl.ds(row_start(j, n_row, half), half)
                for k in range(CORES):
                    source = mine_ref if k == c else other_ref
                    to = j * tr + k * half
                    x_ref[to : to + half, :] = source[at, :]

    q = jnp.concatenate([q_ref[...] for q_ref in q_refs], axis=0)
    ds = pl.ds(pl.multiple_of(pl.program_id(0) * block, block), block)
    out_ref[...] = scaling * lax.dot_general(
        x_ref[:, ds], q, (((0,), (0,)), ((), ())), preferred_element_type=jnp.float32
    )


def wgrad(q_parts, x_mine, x_other, scaling):
    n_row = len(q_parts)
    tr, f_local = q_parts[0].shape
    tokens, d_local = tr * n_row, x_mine.shape[1]
    block = largest_block(d_local, 512)
    vmem = pl.BlockSpec(memory_space=pltpu.VMEM)
    return pl.pallas_call(
        functools.partial(wgrad_kernel, n_row, scaling),
        grid=(d_local // block,),
        out_shape=jax.ShapeDtypeStruct((d_local, f_local), jnp.float32),
        in_specs=[vmem] * (n_row + 2),
        out_specs=pl.BlockSpec((block, f_local), lambda i: (i, 0)),
        scratch_shapes=[pltpu.VMEM((tokens, d_local), jnp.bfloat16)],
        name="wgrad",
        cost_estimate=pl.CostEstimate(
            flops=2 * tokens * d_local * f_local,
            bytes_accessed=4 * d_local * f_local,
            transcendentals=0,
        ),
        compiler_params=pltpu.CompilerParams(vmem_limit_bytes=VMEM_WGRAD * MIB),
    )(*q_parts, x_mine, x_other)


def shards(activations, up_weight, out_grad, round_seed, counter_base):
    n_row, n_col = lax.axis_size("row"), lax.axis_size("col")
    n_chip = n_col // CORES
    assert n_col % (CORES * n_row) == 0
    per_col, d_local = activations.shape
    tokens = per_col * n_col
    chips = [[chip * CORES + c for chip in range(n_chip)] for c in range(CORES)]
    swap = [(i, i ^ 1) for i in range(n_col)]

    own = stochastic_round(out_grad, counter_base, round_seed, per_col)
    q_parts = [own] + [
        lax.ppermute(own, "row", [(i, (i + j) % n_row) for i in range(n_row)])
        for j in range(1, n_row)
    ]
    copies = jnp.broadcast_to(activations, (n_chip, per_col, d_local))
    x_mine = lax.all_to_all(copies, "col", 0, 0, axis_index_groups=chips)
    x_mine = x_mine.reshape(n_chip * per_col, d_local)
    x_other = lax.ppermute(x_mine, "col", swap)
    keep, give = project(q_parts, up_weight)
    taken = lax.ppermute(give, "col", swap)
    pair = keep.astype(jnp.float32) + taken.astype(jnp.float32)
    pair = pair.astype(jnp.bfloat16).reshape(n_chip, per_col, d_local)
    shares = lax.all_to_all(pair, "col", 0, 0, axis_index_groups=chips)
    weight_grad = wgrad(q_parts, x_mine, x_other, tokens ** (-0.5))
    input_grad = jnp.sum(shares.astype(jnp.float32), axis=0)
    return weight_grad, input_grad.astype(jnp.bfloat16)


def solution(mesh):
    placed = (P("col", "row"), P("row", "col"), P("row", "col"), P(), P("row"))
    return jax.shard_map(
        shards,
        mesh=mesh,
        in_specs=placed,
        out_specs=(P("row", "col"), P("col", "row")),
        check_vma=False,
    )
```

time: 131 us -> 75.6 us (0.58)
  local copies, waits for them, and re-layouts: 50.1 us -> 3.32 us
  matrix products: 37.8 us -> 0 us
  Pallas kernels: 0 us -> 30.2 us
  blocking collectives: 13.5 us -> 0 us
  between operations: 14.7 us -> 1.32 us
  waiting for transfers between devices: 12.8 us -> 25.9 us
  starting transfers between devices: 0.08 us -> 12.8 us
    unnamed x1 -> x4, local copies, waits for them, and re-layouts: 50.1 us -> 1.66 us
    dot_general x2 -> x0, matrix products: 37.8 us -> none  [the longest x1 22.8 us: contract(): lax.dot_general(left, right, (((0,), (0,)), ((), ())), preferred_element_...]
    pallas_call x0 -> x3, Pallas kernels: none -> 30.2 us  [the longest x1 18.6 us: wgrad(): pl.pallas_call(functools.partial(wgrad_kernel, n_row, scaling), grid=(d_l...]
    all_to_all x0 -> x2, waiting for transfers between devices: none -> 14.2 us  [the longest x1 14.2 us: shards(): x_mine = lax.all_to_all(copies, 'col', 0, 0, axis_index_groups=chips)]
    all_gather x1 -> x0, blocking collectives: 13.5 us -> none  [shards(): everything = lax.all_gather(quantized, 'row', axis=0, tiled=True)]
    all_gather x1 -> x0, waiting for transfers between devices: 12.1 us -> none  [fold_panels(): everyone = lax.all_gather(activations, 'col', axis=0, tiled=True)]
    ppermute x0 -> x3, waiting for transfers between devices: none -> 11.7 us  [the longest x1 9.82 us: shards(): lax.ppermute(own, 'row', [(i, (i + j) % n_row) for i in range(n_row)])]
    all_to_all x0 -> x2, starting transfers between devices: none -> 9.72 us  [the longest x1 6.08 us: shards(): x_mine = lax.all_to_all(copies, 'col', 0, 0, axis_index_groups=chips)]
  transfers between devices with their start and end apart: 2 -> 5, of which waited for: 1 -> 3; matrix products, arithmetic and copies ran while one was open for 69% -> 3% of each run, Pallas kernels for 0% -> 25%
where the time goes in v1:
time: 75.6 us; the launch traced here: 75.2 us
  Pallas kernels  30.2 us (40%)
  waiting for transfers between devices  25.9 us (34%)
  starting transfers between devices  12.8 us (17%)
  local copies, waits for them, and re-layouts  3.32 us (4%)
  other arithmetic  1.62 us (2%)
  between operations  1.32 us (2%)
    pallas_call x1, Pallas kernels, wgrad(): pl.pallas_call(functools.partial(wgrad_kernel, n_row, scaling), grid=(d_l...  18.6 us
    all_to_all x1, waiting for transfers between devices, shards(): x_mine = lax.all_to_all(copies, 'col', 0, 0, axis_index_groups=chips)  14.2 us
    pallas_call x1, Pallas kernels, project(): pl.pallas_call(functools.partial(project_kernel, n_row, block), out_shape...  11.1 us
    ppermute x1, waiting for transfers between devices, shards(): lax.ppermute(own, 'row', [(i, (i + j) % n_row) for i in range(n_row)])  9.82 us
    all_to_all x1, starting transfers between devices, shards(): x_mine = lax.all_to_all(copies, 'col', 0, 0, axis_index_groups=chips)  6.08 us
    all_to_all x1, starting transfers between devices, shards(): shares = lax.all_to_all(pair, 'col', 0, 0, axis_index_groups=chips)  3.64 us
    ppermute x1, starting transfers between devices, shards(): lax.ppermute(own, 'row', [(i, (i + j) % n_row) for i in range(n_row)])  3.03 us
    ppermute x1, waiting for transfers between devices, shards(): x_other = lax.ppermute(x_mine, 'col', swap)  1.9 us
  transfers between devices with their start and end apart: 5, of which 3 were waited for; matrix products, arithmetic and copies ran while one was open for 3% of the time, Pallas kernels for 25%

profile of v1, /device:TPU:0, one launch (start us, length us, event | category | flops | bytes accessed | tf_op | source)
XLA Modules:
  0.0 75.2 jit_solution(2909825101818074893)
XLA Ops:
  1.3 0.0 copy-start
  1.3 1.0 %copy-done = bf16[64,3328]{1,0:T(8,128)(2,1)S(1)} copy-done((bf16[64,3328]{1,0:T(8,128)(2,1)S(1)}, bf16[64,3328]{1,0:T(8,128)(2,1)}, u32[]{:S(2)}) %copy-start) | copy-done | bytes 426008
  2.3 0.0 copy-start.1
  2.3 0.7 copy-done.1
  2.9 0.6 quantize.1.refs_0_
  3.5 3.0 %collective-permute-start = (bf16[64,3328]{1,0:T(8,128)(2,1)S(1)}, bf16[64,3328]{1,0:T(8,128)(2,1)S(1)}, u32[]{:S(2)}, u32[]{:S(2)}) collective-permute-start(bf16[64,3328]{1,0:T(8,128)(2,1)S(1)} %quantize.1.refs_0_), channel_id=1, source_target_pairs={{0,16},{16,0},{1,17},{17,1},{2,18},{18,2},{3,19},{19,3},{4,20},{20... | collective-permute-start | bytes 1277960 | tf_op jit(solution)/shard_map/ppermute | solution.py:185
  6.6 9.8 %collective-permute-done.refs_1_ = bf16[64,3328]{1,0:T(8,128)(2,1)S(1)} collective-permute-done((bf16[64,3328]{1,0:T(8,128)(2,1)S(1)}, bf16[64,3328]{1,0:T(8,128)(2,1)S(1)}, u32[]{:S(2)}, u32[]{:S(2)}) %collective-permute-start) | collective-permute-done | bytes 426016 | tf_op jit(solution)/shard_map/ppermute | solution.py:185
  16.4 11.1 %project.1 = (bf16[64,4096]{1,0:T(8,128)(2,1)S(1)}, bf16[64,4096]{1,0:T(8,128)(2,1)S(1)}) custom-call(bf16[64,3328]{1,0:T(8,128)(2,1)S(1)} %quantize.1.refs_0_, bf16[64,3328]{1,0:T(8,128)(2,1)S(1)} %collective-permute-done.refs_1_, bf16[4096,3328]{1,0:T(8,128)(2,1)} %refs_2_.1), custom_call_target="tpu_custom_call" | custom-call | flops 3489660928 | bytes 27262976 | tf_op jit(solution)/shard_map/project/pallas_call | solution.py:104
  27.5 0.1 collective-permute-start.2
  27.5 1.7 %broadcast_in_dim.7 = bf16[8,8,4096]{2,1,0:T(8,128)(2,1)} broadcast(bf16[8,4096]{1,0:T(8,128)(2,1)} %param.5), dimensions={1,2} | broadcast | bytes 589824 | tf_op jit(solution)/shard_map/broadcast_in_dim | solution.py:188
  29.2 6.1 %all-to-all-start = ((bf16[8,8,4096]{2,1,0:T(8,128)(2,1)}), bf16[8,8,4096]{2,1,0:T(8,128)(2,1)S(1)}, u32[]{:S(2)}, u32[]{:S(2)}) async-start(bf16[8,8,4096]{2,1,0:T(8,128)(2,1)} %broadcast_in_dim.7), calls=%async_computation | async-start | bytes 1048576 | tf_op jit(solution)/shard_map/all_to_all | solution.py:189
  35.3 0.0 collective-permute-done.2
  35.3 0.9 %fusion = bf16[8,8,4096]{2,1,0:T(8,128)(2,1)} fusion(bf16[64,4096]{1,0:T(8,128)(2,1)S(1)} %collective-permute-done.2, bf16[64,4096]{1,0:T(8,128)(2,1)S(1)} %get-tuple-element.4), kind=kLoop, calls=%fused_computation.1 | loop fusion | flops 1048576 | bytes 1572864 | tf_op jit(solution)/shard_map/reshape | solution.py:195
  36.2 14.2 %all-to-all-done = bf16[8,8,4096]{2,1,0:T(8,128)(2,1)S(1)} async-done(((bf16[8,8,4096]{2,1,0:T(8,128)(2,1)}), bf16[8,8,4096]{2,1,0:T(8,128)(2,1)S(1)}, u32[]{:S(2)}, u32[]{:S(2)}) %all-to-all-start) | async-done | bytes 524320 | tf_op jit(solution)/shard_map/all_to_all | solution.py:189
  50.4 3.6 %all-to-all-start.1 = ((bf16[8,8,4096]{2,1,0:T(8,128)(2,1)}), bf16[8,8,4096]{2,1,0:T(8,128)(2,1)S(1)}, u32[]{:S(2)}, u32[]{:S(2)}) async-start(bf16[8,8,4096]{2,1,0:T(8,128)(2,1)} %fusion), calls=%async_computation.1 | async-start | bytes 1048576 | tf_op jit(solution)/shard_map/all_to_all | solution.py:196
  54.1 0.0 collective-permute-start.1
  54.1 1.9 %collective-permute-done.1.refs_3_ = bf16[64,4096]{1,0:T(8,128)(2,1)S(1)} collective-permute-done((bf16[64,4096]{1,0:T(8,128)(2,1)S(1)}, bf16[64,4096]{1,0:T(8,128)(2,1)S(1)}, u32[]{:S(2)}, u32[]{:S(2)}) %collective-permute-start.1) | collective-permute-done | bytes 524320 | tf_op jit(solution)/shard_map/ppermute | solution.py:191
  56.0 18.6 %wgrad.1 = f32[4096,3328]{1,0:T(8,128)} custom-call(bf16[64,3328]{1,0:T(8,128)(2,1)S(1)} %quantize.1.refs_0_, bf16[64,3328]{1,0:T(8,128)(2,1)S(1)} %collective-permute-done.refs_1_, bf16[64,4096]{1,0:T(8,128)(2,1)S(1)} %bitcast.5, bf16[64,4096]{1,0:T(8,128)(2,1)S(1)} %collective-permute-done.1.refs_3_), custom_call_target="tpu_custom_call" | custom-call | flops 3489660928 | bytes 54525952 | tf_op jit(solution)/shard_map/wgrad/pallas_call | solution.py:157
  74.5 0.0 all-to-all-done.1
  74.5 0.7 reduce_sum.12
Async XLA Ops:
  1.3 1.0 %copy-start = (bf16[64,3328]{1,0:T(8,128)(2,1)S(1)}, bf16[64,3328]{1,0:T(8,128)(2,1)}, u32[]{:S(2)}) copy-start(bf16[64,3328]{1,0:T(8,128)(2,1)} %grad_ref.1) | copy-start | bytes 1277956
  2.3 0.7 copy-start.1
  3.5 12.8 %collective-permute-start = (bf16[64,3328]{1,0:T(8,128)(2,1)S(1)}, bf16[64,3328]{1,0:T(8,128)(2,1)S(1)}, u32[]{:S(2)}, u32[]{:S(2)}) collective-permute-start(bf16[64,3328]{1,0:T(8,128)(2,1)S(1)} %quantize.1.refs_0_), channel_id=1, source_target_pairs={{0,16},{16,0},{1,17},{17,1},{2,18},{18,2},{3,19},{19,3},{4,20},{20... | collective-permute-start | bytes 1277960 | tf_op jit(solution)/shard_map/ppermute | solution.py:185
  27.5 7.8 %collective-permute-start.2 = (bf16[64,4096]{1,0:T(8,128)(2,1)S(1)}, bf16[64,4096]{1,0:T(8,128)(2,1)S(1)}, u32[]{:S(2)}, u32[]{:S(2)}) collective-permute-start(bf16[64,4096]{1,0:T(8,128)(2,1)S(1)} %get-tuple-element.5), channel_id=1, source_target_pairs={{0,1},{1,0},{2,3},{3,2},{4,5},{5,4},{6,7},{7,6},{8,9},{9,8},{10,11... | collective-permute-start | bytes 1572872 | tf_op jit(solution)/shard_map/ppermute | solution.py:193
  29.2 21.2 %all-to-all-start = ((bf16[8,8,4096]{2,1,0:T(8,128)(2,1)}), bf16[8,8,4096]{2,1,0:T(8,128)(2,1)S(1)}, u32[]{:S(2)}, u32[]{:S(2)}) async-start(bf16[8,8,4096]{2,1,0:T(8,128)(2,1)} %broadcast_in_dim.7), calls=%async_computation | async-start | bytes 1048576 | tf_op jit(solution)/shard_map/all_to_all | solution.py:189
  50.4 24.1 %all-to-all-start.1 = ((bf16[8,8,4096]{2,1,0:T(8,128)(2,1)}), bf16[8,8,4096]{2,1,0:T(8,128)(2,1)S(1)}, u32[]{:S(2)}, u32[]{:S(2)}) async-start(bf16[8,8,4096]{2,1,0:T(8,128)(2,1)} %fusion), calls=%async_computation.1 | async-start | bytes 1048576 | tf_op jit(solution)/shard_map/all_to_all | solution.py:196
  54.1 1.9 %collective-permute-start.1 = (bf16[64,4096]{1,0:T(8,128)(2,1)S(1)}, bf16[64,4096]{1,0:T(8,128)(2,1)S(1)}, u32[]{:S(2)}, u32[]{:S(2)}) collective-permute-start(bf16[64,4096]{1,0:T(8,128)(2,1)S(1)} %bitcast.4), channel_id=1, source_target_pairs={{0,1},{1,0},{2,3},{3,2},{4,5},{5,4},{6,7},{7,6},{8,9},{9,8},{10,11... | collective-permute-start | bytes 1572872 | tf_op jit(solution)/shard_map/ppermute | solution.py:191

commit v2 on v1

v2 whole, which is shorter than its diff:
```python
import functools

import jax
import jax.numpy as jnp
from jax import lax
from jax.experimental import pallas as pl
from jax.experimental.pallas import tpu as pltpu
from jax.sharding import PartitionSpec as P


CORES = 2
LANES = 256
MIB = 2**20


def round_kernel(per_col, cuts, seed_ref, base_hbm, grad_hbm, x_hbm, *refs):
    n_cut = len(cuts) - 1
    out_refs, refs = refs[:n_cut], refs[n_cut:]
    copies_hbm, base_ref, grad_ref, x_ref, sems, copy_sems = refs
    loads = [
        pltpu.make_async_copy(base_hbm, base_ref, sems.at[0]),
        pltpu.make_async_copy(x_hbm, x_ref, sems.at[1]),
        pltpu.make_async_copy(grad_hbm, grad_ref, sems.at[2]),
    ]
    for load in loads:
        load.start()
    stores = [
        pltpu.make_async_copy(x_ref, copies_hbm.at[i], copy_sems.at[i])
        for i in range(copies_hbm.shape[0])
    ]
    loads[0].wait()
    rows, f_local = grad_ref.shape
    shape = (rows, rows)
    diagonal = lax.broadcasted_iota(jnp.int32, shape, 0) == lax.broadcasted_iota(
        jnp.int32, shape, 1
    )
    base = jnp.where(diagonal, jnp.broadcast_to(base_ref[...], shape), 0)
    base = jnp.sum(base, axis=1, keepdims=True)
    col_first = lax.axis_index("col") * f_local
    offset = seed_ref[0] * jnp.int32(1013904223)
    loads[1].wait()
    for store in stores:
        store.start()
    loads[2].wait()
    for out_ref, cut, end in zip(out_refs, cuts, cuts[1:], strict=False):
        width = largest_block(end - cut, 256)
        for start in range(cut, end, width):
            columns = lax.broadcasted_iota(jnp.int32, (rows, width), 1)
            counter = base + (columns + (col_first + start))
            mixed = counter * jnp.int32(747796405) + offset
            mixed = mixed ^ (mixed >> 15)
            mixed = mixed * jnp.int32(277803737)
            mixed = mixed ^ (mixed >> 16)
            level = (mixed & 255).astype(jnp.float32)
            grad = grad_ref[:, start : start + width].astype(jnp.float32)
            done = jnp.floor(grad * 4.0 + (level + 0.5) / 256.0) / 4.0
            pieces = [done[i : i + per_col] for i in range(0, rows, per_col)]
            pieces = [p for c in range(CORES) for p in pieces[c::CORES]]
            at = slice(start - cut, start - cut + width)
            out_ref[:, at] = jnp.concatenate(pieces).astype(out_ref.dtype)
    for store in stores:
        store.wait()


def stochastic_round(grad, counter_base, round_seed, activations, cuts, n_chip):
    per_col, d_local = activations.shape
    rows = grad.shape[0]
    vmem = pl.BlockSpec(memory_space=pltpu.VMEM)
    hbm = pl.BlockSpec(memory_space=pltpu.HBM)
    *parts, copies = pl.pallas_call(
        functools.partial(round_kernel, per_col, cuts),
        out_shape=[
            jax.ShapeDtypeStruct((rows, end - cut), jnp.bfloat16)
            for cut, end in zip(cuts, cuts[1:], strict=False)
        ]
        + [jax.ShapeDtypeStruct((n_chip, per_col, d_local), activations.dtype)],
        in_specs=[pl.BlockSpec(memory_space=pltpu.SMEM)] + [hbm] * 3,
        out_specs=[vmem] * (len(cuts) - 1) + [hbm],
        scratch_shapes=[
            pltpu.VMEM((1, rows), jnp.int32),
            pltpu.VMEM(grad.shape, grad.dtype),
            pltpu.VMEM(activations.shape, activations.dtype),
            pltpu.SemaphoreType.DMA((3,)),
            pltpu.SemaphoreType.DMA((n_chip,)),
        ],
        name="quantize",
        cost_estimate=pl.CostEstimate(
            flops=16 * grad.size, bytes_accessed=4 * grad.size, transcendentals=0
        ),
        compiler_params=pltpu.CompilerParams(vmem_limit_bytes=8 * MIB),
    )(round_seed, *in_hbm(counter_base[None, :], grad, activations))
    return parts, copies


def in_hbm(*arrays):
    return [pltpu.with_memory_space_constraint(a, pltpu.HBM) for a in arrays]


def largest_block(length, most):
    return next(b for b in range(min(most, length), 0, -1) if length % b == 0)


def row_start(j, rows, size):
    owner = lax.rem(lax.axis_index("row") - j + rows, rows)
    return pl.multiple_of(owner * size, size)


def project_kernel(n_row, first, final, f_from, block, *refs):
    q_refs, refs = refs[:n_row], refs[n_row:]
    acc_ref = None
    if not first:
        acc_ref, refs = refs[0], refs[1:]
    w_hbm, *outs, w_ref, sems = refs
    tr, f_len = q_refs[0].shape
    half = tr // CORES
    core = lax.rem(lax.axis_index("col"), CORES)

    def fetch(step):
        ds = pl.ds(pl.multiple_of(step * block, block), block)
        return pltpu.make_async_copy(
            w_hbm.at[ds, pl.ds(f_from, f_len)], w_ref.at[ds, :], sems.at[step]
        )

    steps = w_ref.shape[0] // block
    for step in range(steps):
        fetch(step).start()

    @pl.loop(0, steps)
    def _(step):
        fetch(step).wait()
        ds = pl.ds(pl.multiple_of(step * block, block), block)
        q = jnp.concatenate([q_ref[...] for q_ref in q_refs], axis=0)
        part = lax.dot_general(
            w_ref[ds, :], q, (((1,), (1,)), ((), ())), preferred_element_type=jnp.float32
        )
        if acc_ref is not None:
            part = part + acc_ref[ds, :]
        if not final:
            outs[0][ds, :] = part
            return
        whole = part.T.astype(jnp.bfloat16)
        for c in range(CORES):

            @pl.when(core == c)
            def _():
                for j in range(n_row):
                    at = pl.ds(row_start(j, n_row, half), half)
                    for k in range(CORES):
                        piece = whole[j * tr + k * half : j * tr + (k + 1) * half]
                        outs[0 if k == c else 1][at, ds] = piece


def project(q_parts, up_weight, acc, f_from, final):
    n_row = len(q_parts)
    tr, f_len = q_parts[0].shape
    tokens = tr * n_row
    d_local = up_weight.shape[0]
    block = largest_block(d_local, 512)
    vmem = pl.BlockSpec(memory_space=pltpu.VMEM)
    if final:
        out = [jax.ShapeDtypeStruct((tokens // CORES, d_local), jnp.bfloat16)] * 2
    else:
        out = [jax.ShapeDtypeStruct((d_local, tokens), jnp.float32)]
    held = [] if acc is None else [acc]
    return pl.pallas_call(
        functools.partial(project_kernel, n_row, acc is None, final, f_from, block),
        out_shape=out,
        in_specs=[vmem] * (n_row + len(held)) + [pl.BlockSpec(memory_space=pltpu.HBM)],
        out_specs=[vmem] * len(out),
        scratch_shapes=[
            pltpu.VMEM((d_local, f_len), up_weight.dtype),
            pltpu.SemaphoreType.DMA((d_local // block,)),
        ],
        name="project",
        cost_estimate=pl.CostEstimate(
            flops=2 * tokens * d_local * f_len,
            bytes_accessed=2 * d_local * f_len,
            transcendentals=0,
        ),
        compiler_params=pltpu.CompilerParams(vmem_limit_bytes=VMEM_PROJECT * MIB),
    )(*q_parts, *held, *in_hbm(up_weight))


VMEM_PROJECT = 24
VMEM_WGRAD = 32


def wgrad_kernel(n_row, n_cut, scaling, *refs):
    q_refs, refs = refs[: n_row * n_cut], refs[n_row * n_cut :]
    mine_ref, other_ref, out_hbm, x_ref, q_ref, held, sems = refs
    tr = q_refs[0].shape[0]
    half = tr // CORES
    slots, block, _ = held.shape
    core = lax.rem(lax.axis_index("col"), CORES)
    for c in range(CORES):

        @pl.when(core == c)
        def _():
            for j in range(n_row):
                at = pl.ds(row_start(j, n_row, half), half)
                for k in range(CORES):
                    source = mine_ref if k == c else other_ref
                    to = j * tr + k * half
                    x_ref[to : to + half, :] = source[at, :]

    for j in range(n_row):
        start = 0
        for i in range(n_cut):
            part = q_refs[i * n_row + j]
            end = start + part.shape[1]
            q_ref[j * tr : (j + 1) * tr, start:end] = part[...]
            start = end

    def store(step):
        slot = lax.rem(step, slots)
        ds = pl.ds(pl.multiple_of(step * block, block), block)
        return pltpu.make_async_copy(held.at[slot], out_hbm.at[ds, :], sems.at[slot])

    steps = out_hbm.shape[0] // block

    @pl.loop(0, steps)
    def _(step):
        @pl.when(step >= slots)
        def _():
            store(step - slots).wait()

        ds = pl.ds(pl.multiple_of(step * block, block), block)
        held[lax.rem(step, slots)] = scaling * lax.dot_general(
            x_ref[:, ds],
            q_ref[...],
            (((0,), (0,)), ((), ())),
            preferred_element_type=jnp.float32,
        )
        store(step).start()

    for step in range(max(steps - slots, 0), steps):
        store(step).wait()


def wgrad(q_cuts, x_mine, x_other, scaling):
    n_cut, n_row = len(q_cuts), len(q_cuts[0])
    tr = q_cuts[0][0].shape[0]
    f_local = sum(parts[0].shape[1] for parts in q_cuts)
    tokens, d_local = tr * n_row, x_mine.shape[1]
    block = largest_block(d_local, 256)
    slots = min(3, d_local // block)
    vmem = pl.BlockSpec(memory_space=pltpu.VMEM)
    return pl.pallas_call(
        functools.partial(wgrad_kernel, n_row, n_cut, scaling),
        out_shape=jax.ShapeDtypeStruct((d_local, f_local), jnp.float32),
        in_specs=[vmem] * (n_row * n_cut + 2),
        out_specs=pl.BlockSpec(memory_space=pltpu.HBM),
        scratch_shapes=[
            pltpu.VMEM((tokens, d_local), jnp.bfloat16),
            pltpu.VMEM((tokens, f_local), jnp.bfloat16),
            pltpu.VMEM((slots, block, f_local), jnp.float32),
            pltpu.SemaphoreType.DMA((slots,)),
        ],
        name="wgrad",
        cost_estimate=pl.CostEstimate(
            flops=2 * tokens * d_local * f_local,
            bytes_accessed=4 * d_local * f_local,
            transcendentals=0,
        ),
        compiler_params=pltpu.CompilerParams(vmem_limit_bytes=VMEM_WGRAD * MIB),
    )(*[part for parts in q_cuts for part in parts], x_mine, x_other)


def shards(activations, up_weight, out_grad, round_seed, counter_base):
    n_row, n_col = lax.axis_size("row"), lax.axis_size("col")
    n_chip = n_col // CORES
    assert n_col % (CORES * n_row) == 0
    per_col, d_local = activations.shape
    tokens = per_col * n_col
    chips = [[chip * CORES + c for chip in range(n_chip)] for c in range(CORES)]
    swap = [(i, i ^ 1) for i in range(n_col)]

    f_local = out_grad.shape[1]
    middle = f_local // (2 * LANES) * LANES
    cuts = (0, middle, f_local)
    shifts = [[(i, (i + j) % n_row) for i in range(n_row)] for j in range(1, n_row)]
    owns, copies = stochastic_round(
        out_grad, counter_base, round_seed, activations, cuts, n_chip
    )
    q_a = [owns[0]] + [lax.ppermute(owns[0], "row", shift) for shift in shifts]
    q_b = [owns[1]] + [lax.ppermute(owns[1], "row", shift) for shift in shifts]
    x_mine = lax.all_to_all(copies, "col", 0, 0, axis_index_groups=chips)
    x_mine = x_mine.reshape(n_chip * per_col, d_local)
    x_other = lax.ppermute(x_mine, "col", swap)
    (acc,) = project(q_a, up_weight, None, 0, False)
    keep, give = project(q_b, up_weight, acc, middle, True)
    taken = lax.ppermute(give, "col", swap)
    pair = keep.astype(jnp.float32) + taken.astype(jnp.float32)
    pair = pair.astype(jnp.bfloat16).reshape(n_chip, per_col, d_local)
    shares = lax.all_to_all(pair, "col", 0, 0, axis_index_groups=chips)
    weight_grad = wgrad((q_a, q_b), x_mine, x_other, tokens ** (-0.5))
    input_grad = jnp.sum(shares.astype(jnp.float32), axis=0)
    return weight_grad, input_grad.astype(jnp.bfloat16)


def solution(mesh):
    placed = (P("col", "row"), P("row", "col"), P("row", "col"), P(), P("row"))
    return jax.shard_map(
        shards,
        mesh=mesh,
        in_specs=placed,
        out_specs=(P("row", "col"), P("col", "row")),
        check_vma=False,
    )
```

time: 75.6 us -> 71.5 us (0.946)
  waiting for transfers between devices: 25.9 us -> 21.8 us
  local copies, waits for them, and re-layouts: 3.32 us -> 0 us
  Pallas kernels: 30.2 us -> 33.3 us
    ppermute x1 -> x2, waiting for transfers between devices: 9.82 us -> 5.67 us  [the longest x1 5.67 us: shards(): q_a = [owns[0]] + [lax.ppermute(owns[0], 'row', shift) for shift in shifts]]
    pallas_call x3 -> x4, Pallas kernels: 30.2 us -> 33.3 us  [the longest x1 18.1 us: wgrad(): pl.pallas_call(functools.partial(wgrad_kernel, n_row, n_cut, scaling), ou...]
    broadcast_in_dim x1 -> x0, local copies, waits for them, and re-layouts: 1.67 us -> none  [shards(): copies = jnp.broadcast_to(activations, (n_chip, per_col, d_local))]
    unnamed x4 -> x0, local copies, waits for them, and re-layouts: 1.66 us -> none
    ppermute x1 -> x2, starting transfers between devices: 3.03 us -> 3.11 us  [the longest x1 3.03 us: shards(): q_a = [owns[0]] + [lax.ppermute(owns[0], 'row', shift) for shift in shifts]]
  transfers between devices with their start and end apart: 5 -> 6, of which waited for: 3 -> 3; matrix products, arithmetic and copies ran while one was open for 3% -> 1% of each run, Pallas kernels for 25% -> 34%
where the time goes in v2:
time: 71.5 us; the launch traced here: 71.2 us
  Pallas kernels  33.3 us (47%)
  waiting for transfers between devices  21.8 us (30%)
  starting transfers between devices  13.1 us (18%)
  other arithmetic  1.62 us (2%)
  between operations  1.35 us (2%)
    pallas_call x1, Pallas kernels, wgrad(): pl.pallas_call(functools.partial(wgrad_kernel, n_row, n_cut, scaling), ou...  18.1 us
    all_to_all x1, waiting for transfers between devices, shards(): x_mine = lax.all_to_all(copies, 'col', 0, 0, axis_index_groups=chips)  14.2 us
    pallas_call x2, Pallas kernels, project(): pl.pallas_call(functools.partial(project_kernel, n_row, acc is None, fina...  13.5 us
    all_to_all x1, starting transfers between devices, shards(): x_mine = lax.all_to_all(copies, 'col', 0, 0, axis_index_groups=chips)  6.31 us
    ppermute x1, waiting for transfers between devices, shards(): q_a = [owns[0]] + [lax.ppermute(owns[0], 'row', shift) for shift in shifts]  5.67 us
    all_to_all x1, starting transfers between devices, shards(): shares = lax.all_to_all(pair, 'col', 0, 0, axis_index_groups=chips)  3.64 us
    ppermute x1, starting transfers between devices, shards(): q_a = [owns[0]] + [lax.ppermute(owns[0], 'row', shift) for shift in shifts]  3.03 us
    ppermute x1, waiting for transfers between devices, shards(): x_other = lax.ppermute(x_mine, 'col', swap)  1.9 us
  transfers between devices with their start and end apart: 6, of which 3 were waited for; matrix products, arithmetic and copies ran while one was open for 1% of the time, Pallas kernels for 34%

profile of v2, /device:TPU:0, one launch (start us, length us, event | category | flops | bytes accessed | tf_op | source)
XLA Modules:
  0.0 71.2 jit_solution(11239507303560777266)
XLA Ops:
  1.3 1.7 %quantize.1 = (bf16[64,1536]{1,0:T(8,128)(2,1)S(1)}, bf16[64,1792]{1,0:T(8,128)(2,1)S(1)}, bf16[8,8,4096]{2,1,0:T(8,128)(2,1)}) custom-call(s32[1]{0:T(128)S(6)} %copy.7.seed_ref, s32[1,64]{1,0:T(1,128)} %bitcast.6, bf16[64,3328]{1,0:T(8,128)(2,1)} %grad_hbm.1, bf16[8,4096]{1,0:T(8,128)(2,1)} %x_hbm.1), custom_call_target="tpu_custom_call" | custom-call | flops 3407872 | bytes 851968 | tf_op jit(solution)/shard_map/quantize/pallas_call | solution.py:70
  3.0 3.0 %collective-permute-start = (bf16[64,1536]{1,0:T(8,128)(2,1)S(1)}, bf16[64,1536]{1,0:T(8,128)(2,1)S(1)}, u32[]{:S(2)}, u32[]{:S(2)}) collective-permute-start(bf16[64,1536]{1,0:T(8,128)(2,1)S(1)} %get-tuple-element.7.refs_0_), channel_id=1, source_target_pairs={{0,16},{16,0},{1,17},{17,1},{2,18},{18,2},{3,19},{19,3},{4,20},{20... | collective-permute-start | bytes 589832 | tf_op jit(solution)/shard_map/ppermute | solution.py:285
  6.0 0.1 collective-permute-start.1
  6.1 5.7 %collective-permute-done.refs_1_ = bf16[64,1536]{1,0:T(8,128)(2,1)S(1)} collective-permute-done((bf16[64,1536]{1,0:T(8,128)(2,1)S(1)}, bf16[64,1536]{1,0:T(8,128)(2,1)S(1)}, u32[]{:S(2)}, u32[]{:S(2)}) %collective-permute-start) | collective-permute-done | bytes 196640 | tf_op jit(solution)/shard_map/ppermute | solution.py:285
  11.8 6.1 %project.2.refs_2_ = f32[4096,128]{1,0:T(8,128)S(1)} custom-call(bf16[64,1536]{1,0:T(8,128)(2,1)S(1)} %get-tuple-element.7.refs_0_, bf16[64,1536]{1,0:T(8,128)(2,1)S(1)} %collective-permute-done.refs_1_, bf16[4096,3328]{1,0:T(8,128)(2,1)} %refs_3_.1), custom_call_target="tpu_custom_call" | custom-call | flops 1610612736 | bytes 12582912 | tf_op jit(solution)/shard_map/project/pallas_call | solution.py:165
  17.9 0.0 collective-permute-done.1.refs_3_.refs_1_
  17.9 7.4 %project.3 = (bf16[64,4096]{1,0:T(8,128)(2,1)S(1)}, bf16[64,4096]{1,0:T(8,128)(2,1)S(1)}) custom-call(bf16[64,1792]{1,0:T(8,128)(2,1)S(1)} %get-tuple-element.8.refs_2_.refs_0_, bf16[64,1792]{1,0:T(8,128)(2,1)S(1)} %collective-permute-done.1.refs_3_.refs_1_, f32[4096,128]{1,0:T(8,128)S(1)} %project.2.refs_2_, bf16[4096,3328]{1,0:T(8,128)(2,1)} %refs_3_.1), custom_call_target="tpu_custom_call" | custom-call | flops 1879048192 | bytes 14680064 | tf_op jit(solution)/shard_map/project/pallas_call | solution.py:165
  25.3 0.1 collective-permute-start.3
  25.4 6.3 %all-to-all-start = ((bf16[8,8,4096]{2,1,0:T(8,128)(2,1)}), bf16[8,8,4096]{2,1,0:T(8,128)(2,1)S(1)}, u32[]{:S(2)}, u32[]{:S(2)}) async-start(bf16[8,8,4096]{2,1,0:T(8,128)(2,1)} %get-tuple-element.9), calls=%async_computation | async-start | bytes 1048576 | tf_op jit(solution)/shard_map/all_to_all | solution.py:287
  31.7 0.0 collective-permute-done.3
  31.7 0.9 %fusion = bf16[8,8,4096]{2,1,0:T(8,128)(2,1)} fusion(bf16[64,4096]{1,0:T(8,128)(2,1)S(1)} %collective-permute-done.3, bf16[64,4096]{1,0:T(8,128)(2,1)S(1)} %get-tuple-element.10), kind=kLoop, calls=%fused_computation.1 | loop fusion | flops 1048576 | bytes 1572864 | tf_op jit(solution)/shard_map/reshape | solution.py:294
  32.6 14.2 %all-to-all-done = bf16[8,8,4096]{2,1,0:T(8,128)(2,1)S(1)} async-done(((bf16[8,8,4096]{2,1,0:T(8,128)(2,1)}), bf16[8,8,4096]{2,1,0:T(8,128)(2,1)S(1)}, u32[]{:S(2)}, u32[]{:S(2)}) %all-to-all-start) | async-done | bytes 524320 | tf_op jit(solution)/shard_map/all_to_all | solution.py:287
  46.8 3.6 %all-to-all-start.1 = ((bf16[8,8,4096]{2,1,0:T(8,128)(2,1)}), bf16[8,8,4096]{2,1,0:T(8,128)(2,1)S(1)}, u32[]{:S(2)}, u32[]{:S(2)}) async-start(bf16[8,8,4096]{2,1,0:T(8,128)(2,1)} %fusion), calls=%async_computation.1 | async-start | bytes 1048576 | tf_op jit(solution)/shard_map/all_to_all | solution.py:295
  50.5 0.0 collective-permute-start.2
  50.5 1.9 %collective-permute-done.2.refs_5_ = bf16[64,4096]{1,0:T(8,128)(2,1)S(1)} collective-permute-done((bf16[64,4096]{1,0:T(8,128)(2,1)S(1)}, bf16[64,4096]{1,0:T(8,128)(2,1)S(1)}, u32[]{:S(2)}, u32[]{:S(2)}) %collective-permute-start.2) | collective-permute-done | bytes 524320 | tf_op jit(solution)/shard_map/ppermute | solution.py:289
  52.4 18.1 %wgrad.1 = f32[4096,3328]{1,0:T(8,128)} custom-call(bf16[64,1536]{1,0:T(8,128)(2,1)S(1)} %get-tuple-element.7.refs_0_, bf16[64,1536]{1,0:T(8,128)(2,1)S(1)} %collective-permute-done.refs_1_, bf16[64,1792]{1,0:T(8,128)(2,1)S(1)} %get-tuple-element.8.refs_2_.refs_0_, bf16[64,1792]{1,0:T(8,128)(2,1)S(1)} %collective-permute-done.1.refs_3_.refs_1_, ...), custom_call_target="tpu_custom_call" | custom-call | flops 3489660928 | bytes 54525952 | tf_op jit(solution)/shard_map/wgrad/pallas_call | solution.py:248
  70.5 0.0 all-to-all-done.1
  70.5 0.7 reduce_sum.12
Async XLA Ops:
  3.0 8.8 %collective-permute-start = (bf16[64,1536]{1,0:T(8,128)(2,1)S(1)}, bf16[64,1536]{1,0:T(8,128)(2,1)S(1)}, u32[]{:S(2)}, u32[]{:S(2)}) collective-permute-start(bf16[64,1536]{1,0:T(8,128)(2,1)S(1)} %get-tuple-element.7.refs_0_), channel_id=1, source_target_pairs={{0,16},{16,0},{1,17},{17,1},{2,18},{18,2},{3,19},{19,3},{4,20},{20... | collective-permute-start | bytes 589832 | tf_op jit(solution)/shard_map/ppermute | solution.py:285
  6.0 11.8 %collective-permute-start.1 = (bf16[64,1792]{1,0:T(8,128)(2,1)S(1)}, bf16[64,1792]{1,0:T(8,128)(2,1)S(1)}, u32[]{:S(2)}, u32[]{:S(2)}) collective-permute-start(bf16[64,1792]{1,0:T(8,128)(2,1)S(1)} %get-tuple-element.8.refs_2_.refs_0_), channel_id=1, source_target_pairs={{0,16},{16,0},{1,17},{17,1},{2,18},{18,2},{3,19},{19,3},{4,20},{20... | collective-permute-start | bytes 688136 | tf_op jit(solution)/shard_map/ppermute | solution.py:286
  25.3 6.4 %collective-permute-start.3 = (bf16[64,4096]{1,0:T(8,128)(2,1)S(1)}, bf16[64,4096]{1,0:T(8,128)(2,1)S(1)}, u32[]{:S(2)}, u32[]{:S(2)}) collective-permute-start(bf16[64,4096]{1,0:T(8,128)(2,1)S(1)} %get-tuple-element.11), channel_id=1, source_target_pairs={{0,1},{1,0},{2,3},{3,2},{4,5},{5,4},{6,7},{7,6},{8,9},{9,8},{10,11... | collective-permute-start | bytes 1572872 | tf_op jit(solution)/shard_map/ppermute | solution.py:292
  25.4 21.4 %all-to-all-start = ((bf16[8,8,4096]{2,1,0:T(8,128)(2,1)}), bf16[8,8,4096]{2,1,0:T(8,128)(2,1)S(1)}, u32[]{:S(2)}, u32[]{:S(2)}) async-start(bf16[8,8,4096]{2,1,0:T(8,128)(2,1)} %get-tuple-element.9), calls=%async_computation | async-start | bytes 1048576 | tf_op jit(solution)/shard_map/all_to_all | solution.py:287
  46.8 23.7 %all-to-all-start.1 = ((bf16[8,8,4096]{2,1,0:T(8,128)(2,1)}), bf16[8,8,4096]{2,1,0:T(8,128)(2,1)S(1)}, u32[]{:S(2)}, u32[]{:S(2)}) async-start(bf16[8,8,4096]{2,1,0:T(8,128)(2,1)} %fusion), calls=%async_computation.1 | async-start | bytes 1048576 | tf_op jit(solution)/shard_map/all_to_all | solution.py:295
  50.5 1.9 %collective-permute-start.2 = (bf16[64,4096]{1,0:T(8,128)(2,1)S(1)}, bf16[64,4096]{1,0:T(8,128)(2,1)S(1)}, u32[]{:S(2)}, u32[]{:S(2)}) collective-permute-start(bf16[64,4096]{1,0:T(8,128)(2,1)S(1)} %bitcast.4), channel_id=1, source_target_pairs={{0,1},{1,0},{2,3},{3,2},{4,5},{5,4},{6,7},{7,6},{8,9},{9,8},{10,11... | collective-permute-start | bytes 1572872 | tf_op jit(solution)/shard_map/ppermute | solution.py:289

commit v3 on v2

v3 whole, which is shorter than its diff:
```python
import functools

import jax
import jax.numpy as jnp
from jax import lax
from jax.experimental import pallas as pl
from jax.experimental.pallas import tpu as pltpu
from jax.sharding import PartitionSpec as P


CORES = 2
LANES = 256
MIB = 2**20


def round_kernel(per_col, cuts, seed_ref, base_hbm, grad_hbm, x_hbm, w_hbm, *refs):
    n_cut = len(cuts) - 1
    out_refs, refs = refs[:n_cut], refs[n_cut:]
    copies_hbm, head_ref, base_ref, grad_ref, x_ref, sems, copy_sems = refs
    loads = [
        pltpu.make_async_copy(x_hbm, x_ref, sems.at[0]),
        pltpu.make_async_copy(base_hbm, base_ref, sems.at[1]),
    ] + [
        pltpu.make_async_copy(
            grad_hbm.at[:, cut:end], grad_ref.at[:, cut:end], sems.at[2 + i]
        )
        for i, (cut, end) in enumerate(zip(cuts, cuts[1:], strict=False))
    ]
    loads.append(
        pltpu.make_async_copy(
            w_hbm.at[: head_ref.shape[0], : head_ref.shape[1]], head_ref, sems.at[1 + len(cuts)]
        )
    )
    for load in loads:
        load.start()
    stores = [
        pltpu.make_async_copy(x_ref, copies_hbm.at[i], copy_sems.at[i])
        for i in range(copies_hbm.shape[0])
    ]
    loads[1].wait()
    rows, f_local = grad_ref.shape
    shape = (rows, rows)
    diagonal = lax.broadcasted_iota(jnp.int32, shape, 0) == lax.broadcasted_iota(
        jnp.int32, shape, 1
    )
    base = jnp.where(diagonal, jnp.broadcast_to(base_ref[...], shape), 0)
    base = jnp.sum(base, axis=1, keepdims=True)
    col_first = lax.axis_index("col") * f_local
    offset = seed_ref[0] * jnp.int32(1013904223)
    loads[0].wait()
    for store in stores:
        store.start()
    for out_ref, load, cut, end in zip(out_refs, loads[2:-1], cuts, cuts[1:], strict=False):
        load.wait()
        width = largest_block(end - cut, 256)
        for start in range(cut, end, width):
            columns = lax.broadcasted_iota(jnp.int32, (rows, width), 1)
            counter = base + (columns + (col_first + start))
            mixed = counter * jnp.int32(747796405) + offset
            mixed = mixed ^ (mixed >> 15)
            mixed = mixed * jnp.int32(277803737)
            mixed = mixed ^ (mixed >> 16)
            level = (mixed & 255).astype(jnp.float32)
            grad = grad_ref[:, start : start + width].astype(jnp.float32)
            done = jnp.floor(grad * 4.0 + (level + 0.5) / 256.0) / 4.0
            pieces = [done[i : i + per_col] for i in range(0, rows, per_col)]
            pieces = [p for c in range(CORES) for p in pieces[c::CORES]]
            at = slice(start - cut, start - cut + width)
            out_ref[:, at] = jnp.concatenate(pieces).astype(out_ref.dtype)
    for store in stores:
        store.wait()
    loads[-1].wait()


def stochastic_round(
    grad, counter_base, round_seed, activations, up_weight, cuts, n_chip
):
    per_col, d_local = activations.shape
    rows = grad.shape[0]
    vmem = pl.BlockSpec(memory_space=pltpu.VMEM)
    hbm = pl.BlockSpec(memory_space=pltpu.HBM)
    *parts, copies, head = pl.pallas_call(
        functools.partial(round_kernel, per_col, cuts),
        out_shape=[
            jax.ShapeDtypeStruct((rows, end - cut), jnp.bfloat16)
            for cut, end in zip(cuts, cuts[1:], strict=False)
        ]
        + [
            jax.ShapeDtypeStruct((n_chip, per_col, d_local), activations.dtype),
            jax.ShapeDtypeStruct((project_block(d_local), cuts[1]), up_weight.dtype),
        ],
        in_specs=[pl.BlockSpec(memory_space=pltpu.SMEM)] + [hbm] * 4,
        out_specs=[vmem] * (len(cuts) - 1) + [hbm, vmem],
        scratch_shapes=[
            pltpu.VMEM((1, rows), jnp.int32),
            pltpu.VMEM(grad.shape, grad.dtype),
            pltpu.VMEM(activations.shape, activations.dtype),
            pltpu.SemaphoreType.DMA((2 + len(cuts),)),
            pltpu.SemaphoreType.DMA((n_chip,)),
        ],
        name="quantize",
        cost_estimate=pl.CostEstimate(
            flops=16 * grad.size, bytes_accessed=4 * grad.size, transcendentals=0
        ),
        compiler_params=pltpu.CompilerParams(vmem_limit_bytes=8 * MIB),
    )(round_seed, *in_hbm(counter_base[None, :], grad, activations, up_weight))
    return parts, copies, head


def in_hbm(*arrays):
    return [pltpu.with_memory_space_constraint(a, pltpu.HBM) for a in arrays]


def largest_block(length, most):
    return next(b for b in range(min(most, length), 0, -1) if length % b == 0)


def row_start(j, rows, size):
    owner = lax.rem(lax.axis_index("row") - j + rows, rows)
    return pl.multiple_of(owner * size, size)


def project_block(d_local):
    return largest_block(d_local, 512)


def project_kernel(n_row, final, f_from, block, *refs):
    q_refs, refs = refs[:n_row], refs[n_row:]
    if final:
        acc_ref, head_ref, w_hbm, keep_ref, give_ref, w_ref, sems, turned_ref = refs
    else:
        head_ref, w_hbm, acc_ref, ahead_ref, w_ref, sems, ahead_sem = refs
    head = head_ref.shape[0] // block
    tr, f_len = q_refs[0].shape
    half = tr // CORES
    core = lax.rem(lax.axis_index("col"), CORES)
    steps = w_ref.shape[0] // block

    def rows_of(step):
        return pl.ds(pl.multiple_of(step * block, block), block)

    def fetch(step):
        source = w_hbm.at[rows_of(step), pl.ds(f_from, f_len)]
        return pltpu.make_async_copy(source, w_ref.at[rows_of(step), :], sems.at[step])

    def multiply(step, weight_ref):
        at_d = rows_of(step)
        part = lax.dot_general(
            weight_ref[at_d, :],
            jnp.concatenate([q_ref[...] for q_ref in q_refs], axis=0),
            (((1,), (1,)), ((), ())),
            preferred_element_type=jnp.float32,
        )
        if not final:
            acc_ref[at_d, :] = part
            return
        turned_ref[...] = (part + acc_ref[at_d, :]).astype(jnp.bfloat16).T
        for j in range(n_row):
            at = pl.ds(row_start(j, n_row, half), half)
            for out_ref, c in ((keep_ref, core), (give_ref, 1 - core)):
                source = pl.multiple_of(j * tr + c * half, half)
                out_ref[at, at_d] = turned_ref[pl.ds(source, half), :]

    for step in range(head, steps):
        fetch(step).start()
    if not final:
        f_next = f_from + f_len
        source = w_hbm.at[: ahead_ref.shape[0], f_next : f_next + ahead_ref.shape[1]]
        ahead = pltpu.make_async_copy(source, ahead_ref, ahead_sem)
        ahead.start()

    @pl.loop(0, head)
    def _(step):
        multiply(step, head_ref)

    @pl.loop(head, steps)
    def _(step):
        fetch(step).wait()
        multiply(step, w_ref)

    if not final:
        ahead.wait()


def project(q_parts, up_weight, f_from, held):
    n_row = len(q_parts)
    tr, f_len = q_parts[0].shape
    tokens = tr * n_row
    d_local, f_local = up_weight.shape
    final = len(held) > 1
    block = project_block(d_local)
    steps = d_local // block
    vmem = pl.BlockSpec(memory_space=pltpu.VMEM)
    scratch = [
        pltpu.VMEM((d_local, f_len), up_weight.dtype),
        pltpu.SemaphoreType.DMA((steps,)),
    ]
    if final:
        scratch.append(pltpu.VMEM((tokens, block), jnp.bfloat16))
        out = [jax.ShapeDtypeStruct((tokens // CORES, d_local), jnp.bfloat16)] * 2
    else:
        ahead = (block * max(1, steps // 4), f_local - f_len)
        out = [
            jax.ShapeDtypeStruct((d_local, tokens), jnp.float32),
            jax.ShapeDtypeStruct(ahead, up_weight.dtype),
        ]
        scratch.append(pltpu.SemaphoreType.DMA(()))
    return pl.pallas_call(
        functools.partial(project_kernel, n_row, final, f_from, block),
        out_shape=out,
        in_specs=[vmem] * (n_row + len(held)) + [pl.BlockSpec(memory_space=pltpu.HBM)],
        out_specs=[vmem] * 2,
        scratch_shapes=scratch,
        name="project",
        cost_estimate=pl.CostEstimate(
            flops=2 * tokens * d_local * f_len,
            bytes_accessed=2 * d_local * f_len,
            transcendentals=0,
        ),
        compiler_params=pltpu.CompilerParams(vmem_limit_bytes=VMEM_PROJECT * MIB),
    )(*q_parts, *held, *in_hbm(up_weight))


VMEM_PROJECT = 28
VMEM_WGRAD = 32


def pair_kernel(keep_ref, taken_ref, out_ref):
    total = keep_ref[...].astype(jnp.float32) + taken_ref[...].astype(jnp.float32)
    out_ref[...] = total.astype(out_ref.dtype)


def pair_sum(keep, taken):
    vmem = pl.BlockSpec(memory_space=pltpu.VMEM)
    return pl.pallas_call(
        pair_kernel,
        out_shape=jax.ShapeDtypeStruct(keep.shape, keep.dtype),
        in_specs=[vmem] * 2,
        out_specs=vmem,
        name="pairsum",
        cost_estimate=pl.CostEstimate(
            flops=keep.size, bytes_accessed=6 * keep.size, transcendentals=0
        ),
        compiler_params=pltpu.CompilerParams(vmem_limit_bytes=8 * MIB),
    )(keep, taken)


def wgrad_kernel(n_row, n_cut, scaling, *refs):
    q_refs, refs = refs[: n_row * n_cut], refs[n_row * n_cut :]
    mine_ref, other_ref, out_hbm, x_ref, q_ref, held, sems = refs
    tr = q_refs[0].shape[0]
    half = tr // CORES
    slots, block, _ = held.shape
    core = lax.rem(lax.axis_index("col"), CORES)
    for c in range(CORES):

        @pl.when(core == c)
        def _():
            for j in range(n_row):
                at = pl.ds(row_start(j, n_row, half), half)
                for k in range(CORES):
                    source = mine_ref if k == c else other_ref
                    to = j * tr + k * half
                    x_ref[to : to + half, :] = source[at, :]

    for j in range(n_row):
        start = 0
        for i in range(n_cut):
            part = q_refs[i * n_row + j]
            end = start + part.shape[1]
            q_ref[j * tr : (j + 1) * tr, start:end] = part[...]
            start = end

    f_local = out_hbm.shape[1]
    cuts = (0, f_local // (2 * LANES) * LANES, f_local)
    sides = [slice(*side) for side in zip(cuts, cuts[1:], strict=False)]

    def store(step, side):
        slot = lax.rem(step, slots)
        rows = pl.ds(pl.multiple_of(step * block, block), block)
        return pltpu.make_async_copy(
            held.at[slot, :, sides[side]], out_hbm.at[rows, sides[side]], sems.at[slot, side]
        )

    steps = out_hbm.shape[0] // block

    @pl.loop(0, steps)
    def _(step):
        rows = pl.ds(pl.multiple_of(step * block, block), block)
        for side in range(len(sides)):

            @pl.when(step >= slots)
            def _():
                store(step - slots, side).wait()

            held[lax.rem(step, slots), :, sides[side]] = scaling * lax.dot_general(
                x_ref[:, rows],
                q_ref[:, sides[side]],
                (((0,), (0,)), ((), ())),
                preferred_element_type=jnp.float32,
            )
            store(step, side).start()

    for step in range(max(steps - slots, 0), steps):
        for side in range(len(sides)):
            store(step, side).wait()


def wgrad(q_cuts, x_mine, x_other, scaling):
    n_cut, n_row = len(q_cuts), len(q_cuts[0])
    tr = q_cuts[0][0].shape[0]
    f_local = sum(parts[0].shape[1] for parts in q_cuts)
    tokens, d_local = tr * n_row, x_mine.shape[1]
    block = largest_block(d_local, 256)
    slots = min(3, d_local // block)
    vmem = pl.BlockSpec(memory_space=pltpu.VMEM)
    return pl.pallas_call(
        functools.partial(wgrad_kernel, n_row, n_cut, scaling),
        out_shape=jax.ShapeDtypeStruct((d_local, f_local), jnp.float32),
        in_specs=[vmem] * (n_row * n_cut + 2),
        out_specs=pl.BlockSpec(memory_space=pltpu.HBM),
        scratch_shapes=[
            pltpu.VMEM((tokens, d_local), jnp.bfloat16),
            pltpu.VMEM((tokens, f_local), jnp.bfloat16),
            pltpu.VMEM((slots, block, f_local), jnp.float32),
            pltpu.SemaphoreType.DMA((slots, 2)),
        ],
        name="wgrad",
        cost_estimate=pl.CostEstimate(
            flops=2 * tokens * d_local * f_local,
            bytes_accessed=4 * d_local * f_local,
            transcendentals=0,
        ),
        compiler_params=pltpu.CompilerParams(vmem_limit_bytes=VMEM_WGRAD * MIB),
    )(*[part for parts in q_cuts for part in parts], x_mine, x_other)


def shards(activations, up_weight, out_grad, round_seed, counter_base):
    n_row, n_col = lax.axis_size("row"), lax.axis_size("col")
    n_chip = n_col // CORES
    assert n_col % (CORES * n_row) == 0
    per_col, d_local = activations.shape
    tokens = per_col * n_col
    chips = [[chip * CORES + c for chip in range(n_chip)] for c in range(CORES)]
    swap = [(i, i ^ 1) for i in range(n_col)]

    f_local = out_grad.shape[1]
    middle = f_local // (2 * LANES) * LANES
    cuts = (0, middle, f_local)
    shifts = [[(i, (i + j) % n_row) for i in range(n_row)] for j in range(1, n_row)]
    owns, copies, head = stochastic_round(
        out_grad, counter_base, round_seed, activations, up_weight, cuts, n_chip
    )
    q_a = [owns[0]] + [lax.ppermute(owns[0], "row", shift) for shift in shifts]
    q_b = [owns[1]] + [lax.ppermute(owns[1], "row", shift) for shift in shifts]
    x_mine = lax.all_to_all(copies, "col", 0, 0, axis_index_groups=chips)
    x_mine = x_mine.reshape(n_chip * per_col, d_local)
    x_other = lax.ppermute(x_mine, "col", swap)
    held = project(q_a, up_weight, 0, (head,))
    keep, give = project(q_b, up_weight, middle, held)
    taken = lax.ppermute(give, "col", swap)
    pair = pair_sum(keep, taken).reshape(n_chip, per_col, d_local)
    shares = lax.all_to_all(pair, "col", 0, 0, axis_index_groups=chips)
    weight_grad = wgrad((q_a, q_b), x_mine, x_other, tokens ** (-0.5))
    input_grad = jnp.sum(shares.astype(jnp.float32), axis=0)
    return weight_grad, input_grad.astype(jnp.bfloat16)


def solution(mesh):
    placed = (P("col", "row"), P("row", "col"), P("row", "col"), P(), P("row"))
    return jax.shard_map(
        shards,
        mesh=mesh,
        in_specs=placed,
        out_specs=(P("row", "col"), P("col", "row")),
        check_vma=False,
    )
```

time: 71.5 us -> 53.5 us (0.75)
  waiting for transfers between devices: 21.8 us -> 3.81 us
  starting transfers between devices: 13.1 us -> 15.5 us
  Pallas kernels: 33.3 us -> 31.9 us
  other arithmetic: 1.62 us -> 0.7 us
    all_to_all x1, waiting for transfers between devices: 14.2 us -> 0.01 us  [shards(): x_mine = lax.all_to_all(copies, 'col', 0, 0, axis_index_groups=chips)]
    ppermute x1, waiting for transfers between devices: 5.67 us -> 0.01 us  [shards(): q_a = [owns[0]] + [lax.ppermute(owns[0], 'row', shift) for shift in shifts]]
    all_to_all x1, starting transfers between devices: 3.64 us -> 5.99 us  [shards(): shares = lax.all_to_all(pair, 'col', 0, 0, axis_index_groups=chips)]
    ppermute x1, waiting for transfers between devices: 0.01 us -> 1.9 us  [shards(): taken = lax.ppermute(give, 'col', swap)]
    pallas_call x2 -> x3, Pallas kernels: 13.5 us -> 12.3 us  [the longest x2 11.3 us: project(): pl.pallas_call(functools.partial(project_kernel, n_row, final, f_from, bl...]
    reshape x1 -> x0, other arithmetic: 0.91 us -> none  [shards(): pair = pair.astype(jnp.bfloat16).reshape(n_chip, per_col, d_local)]
  transfers between devices with their start and end apart: 6 -> 6, of which waited for: 3 -> 2; matrix products, arithmetic and copies ran while one was open for 1% -> 0% of each run, Pallas kernels for 34% -> 57%
where the time goes in v3:
time: 53.5 us; the launch traced here: 53.2 us
  Pallas kernels  31.9 us (60%)
  starting transfers between devices  15.5 us (29%)
  waiting for transfers between devices  3.81 us (7%)
  between operations  1.35 us (3%)
  other arithmetic  0.7 us (1%)
    pallas_call x1, Pallas kernels, wgrad(): pl.pallas_call(functools.partial(wgrad_kernel, n_row, n_cut, scaling), ou...  17.8 us
    pallas_call x2, Pallas kernels, project(): pl.pallas_call(functools.partial(project_kernel, n_row, final, f_from, bl...  11.3 us
    all_to_all x1, starting transfers between devices, shards(): x_mine = lax.all_to_all(copies, 'col', 0, 0, axis_index_groups=chips)  6.29 us
    all_to_all x1, starting transfers between devices, shards(): shares = lax.all_to_all(pair, 'col', 0, 0, axis_index_groups=chips)  5.99 us
    ppermute x1, starting transfers between devices, shards(): q_a = [owns[0]] + [lax.ppermute(owns[0], 'row', shift) for shift in shifts]  3.03 us
    ppermute x1, waiting for transfers between devices, shards(): x_other = lax.ppermute(x_mine, 'col', swap)  1.9 us
    ppermute x1, waiting for transfers between devices, shards(): taken = lax.ppermute(give, 'col', swap)  1.9 us
    pallas_call x1, Pallas kernels, stochastic_round(): pl.pallas_call(functools.partial(round_kernel, per_col, cuts), out_shape=...  1.8 us
  transfers between devices with their start and end apart: 6, of which 2 were waited for; matrix products, arithmetic and copies ran while one was open for 0% of the time, Pallas kernels for 57%

profile of v3, /device:TPU:0, one launch (start us, length us, event | category | flops | bytes accessed | tf_op | source)
XLA Modules:
  0.0 53.2 jit_solution(4850674772862381305)
XLA Ops:
  1.3 1.8 %quantize.1 = (bf16[64,1536]{1,0:T(8,128)(2,1)S(1)}, bf16[64,1792]{1,0:T(8,128)(2,1)S(1)}, bf16[8,8,4096]{2,1,0:T(8,128)(2,1)}, bf16[512,1536]{1,0:T(8,128)(2,1)S(1)}) custom-call(s32[1]{0:T(128)S(6)} %copy.7.seed_ref, s32[1,64]{1,0:T(1,128)} %bitcast.5, bf16[64,3328]{1,0:T(8,128)(2,1)} %grad_hbm.1, bf16[8,4096]{1,0:T(8,128)(2,1)} %x_hbm.1, ...), custom_call_target="tpu_custom_call" | custom-call | flops 3407872 | bytes 851968 | tf_op jit(solution)/shard_map/quantize/pallas_call | solution.py:82
  3.1 3.0 %collective-permute-start = (bf16[64,1536]{1,0:T(8,128)(2,1)S(1)}, bf16[64,1536]{1,0:T(8,128)(2,1)S(1)}, u32[]{:S(2)}, u32[]{:S(2)}) collective-permute-start(bf16[64,1536]{1,0:T(8,128)(2,1)S(1)} %get-tuple-element.10.refs_0_), channel_id=1, source_target_pairs={{0,16},{16,0},{1,17},{17,1},{2,18},{18,2},{3,19},{19,3},{4,20},{20... | collective-permute-start | bytes 589832 | tf_op jit(solution)/shard_map/ppermute | solution.py:354
  6.1 0.1 collective-permute-start.1
  6.2 6.3 %all-to-all-start = ((bf16[8,8,4096]{2,1,0:T(8,128)(2,1)}), bf16[8,8,4096]{2,1,0:T(8,128)(2,1)S(1)}, u32[]{:S(2)}, u32[]{:S(2)}) async-start(bf16[8,8,4096]{2,1,0:T(8,128)(2,1)} %get-tuple-element.12), calls=%async_computation | async-start | bytes 1048576 | tf_op jit(solution)/shard_map/all_to_all | solution.py:356
  12.5 0.0 collective-permute-done.refs_1_
  12.5 5.5 %project.2 = (f32[4096,128]{1,0:T(8,128)S(1)}, bf16[1024,1792]{1,0:T(8,128)(2,1)S(1)}) custom-call(bf16[64,1536]{1,0:T(8,128)(2,1)S(1)} %get-tuple-element.10.refs_0_, bf16[64,1536]{1,0:T(8,128)(2,1)S(1)} %collective-permute-done.refs_1_, bf16[512,1536]{1,0:T(8,128)(2,1)S(1)} %get-tuple-element.13.refs_2_, bf16[4096,3328]{1,0:T(8,128)(2,1)} %refs_4_.1), custom_call_target="tpu_custom_call" | custom-call | flops 1610612736 | bytes 12582912 | tf_op jit(solution)/shard_map/project/pallas_call | solution.py:208
  18.0 0.0 collective-permute-done.1.refs_3_.refs_1_
  18.0 5.8 %project.3 = (bf16[64,4096]{1,0:T(8,128)(2,1)S(1)}, bf16[64,4096]{1,0:T(8,128)(2,1)S(1)}) custom-call(bf16[64,1792]{1,0:T(8,128)(2,1)S(1)} %get-tuple-element.11.refs_2_.refs_0_, bf16[64,1792]{1,0:T(8,128)(2,1)S(1)} %collective-permute-done.1.refs_3_.refs_1_, f32[4096,128]{1,0:T(8,128)S(1)} %get-tuple-element.14.refs_2_, ...), custom_call_target="tpu_custom_call" | custom-call | flops 1879048192 | bytes 14680064 | tf_op jit(solution)/shard_map/project/pallas_call | solution.py:208
  23.8 0.1 collective-permute-start.3
  23.9 1.9 %collective-permute-done.3.taken_ref = bf16[64,4096]{1,0:T(8,128)(2,1)S(1)} collective-permute-done((bf16[64,4096]{1,0:T(8,128)(2,1)S(1)}, bf16[64,4096]{1,0:T(8,128)(2,1)S(1)}, u32[]{:S(2)}, u32[]{:S(2)}) %collective-permute-start.3) | collective-permute-done | bytes 524320 | tf_op jit(solution)/shard_map/ppermute | solution.py:361
  25.8 0.9 %pairsum.1 = bf16[64,4096]{1,0:T(8,128)(2,1)} custom-call(bf16[64,4096]{1,0:T(8,128)(2,1)S(1)} %get-tuple-element.16.keep_ref, bf16[64,4096]{1,0:T(8,128)(2,1)S(1)} %collective-permute-done.3.taken_ref), custom_call_target="tpu_custom_call" | custom-call | flops 262144 | bytes 1572864 | tf_op jit(solution)/shard_map/pairsum/pallas_call | solution.py:235
  26.7 0.0 all-to-all-done
  26.7 6.0 %all-to-all-start.1 = ((bf16[8,8,4096]{2,1,0:T(8,128)(2,1)}), bf16[8,8,4096]{2,1,0:T(8,128)(2,1)S(1)}, u32[]{:S(2)}, u32[]{:S(2)}) async-start(bf16[8,8,4096]{2,1,0:T(8,128)(2,1)} %bitcast.2), calls=%async_computation.1 | async-start | bytes 1048576 | tf_op jit(solution)/shard_map/all_to_all | solution.py:363
  32.7 0.0 collective-permute-start.2
  32.7 1.9 %collective-permute-done.2.refs_5_ = bf16[64,4096]{1,0:T(8,128)(2,1)S(1)} collective-permute-done((bf16[64,4096]{1,0:T(8,128)(2,1)S(1)}, bf16[64,4096]{1,0:T(8,128)(2,1)S(1)}, u32[]{:S(2)}, u32[]{:S(2)}) %collective-permute-start.2) | collective-permute-done | bytes 524320 | tf_op jit(solution)/shard_map/ppermute | solution.py:358
  34.6 17.8 %wgrad.1 = f32[4096,3328]{1,0:T(8,128)} custom-call(bf16[64,1536]{1,0:T(8,128)(2,1)S(1)} %get-tuple-element.10.refs_0_, bf16[64,1536]{1,0:T(8,128)(2,1)S(1)} %collective-permute-done.refs_1_, bf16[64,1792]{1,0:T(8,128)(2,1)S(1)} %get-tuple-element.11.refs_2_.refs_0_, bf16[64,1792]{1,0:T(8,128)(2,1)S(1)} %collective-permute-done.1.refs_3_.refs_1_, ...), custom_call_target="tpu_custom_call" | custom-call | flops 3489660928 | bytes 54525952 | tf_op jit(solution)/shard_map/wgrad/pallas_call | solution.py:317
  52.5 0.0 all-to-all-done.1
  52.5 0.7 %reduce_sum.12 = bf16[8,4096]{1,0:T(8,128)(2,1)} reduce(bf16[8,8,4096]{2,1,0:T(8,128)(2,1)S(1)} %all-to-all-done.1, bf16[]{:T(256)} %constant.2.clone.1), dimensions={0}, to_apply=%region_0.0 | reduce | flops 229376 | bytes 589826 | tf_op jit(solution)/shard_map/reduce_sum | solution.py:365
Async XLA Ops:
  3.1 9.4 %collective-permute-start = (bf16[64,1536]{1,0:T(8,128)(2,1)S(1)}, bf16[64,1536]{1,0:T(8,128)(2,1)S(1)}, u32[]{:S(2)}, u32[]{:S(2)}) collective-permute-start(bf16[64,1536]{1,0:T(8,128)(2,1)S(1)} %get-tuple-element.10.refs_0_), channel_id=1, source_target_pairs={{0,16},{16,0},{1,17},{17,1},{2,18},{18,2},{3,19},{19,3},{4,20},{20... | collective-permute-start | bytes 589832 | tf_op jit(solution)/shard_map/ppermute | solution.py:354
  6.1 11.9 %collective-permute-start.1 = (bf16[64,1792]{1,0:T(8,128)(2,1)S(1)}, bf16[64,1792]{1,0:T(8,128)(2,1)S(1)}, u32[]{:S(2)}, u32[]{:S(2)}) collective-permute-start(bf16[64,1792]{1,0:T(8,128)(2,1)S(1)} %get-tuple-element.11.refs_2_.refs_0_), channel_id=1, source_target_pairs={{0,16},{16,0},{1,17},{17,1},{2,18},{18,2},{3,19},{19,3},{4,20},{20... | collective-permute-start | bytes 688136 | tf_op jit(solution)/shard_map/ppermute | solution.py:355
  6.2 20.6 %all-to-all-start = ((bf16[8,8,4096]{2,1,0:T(8,128)(2,1)}), bf16[8,8,4096]{2,1,0:T(8,128)(2,1)S(1)}, u32[]{:S(2)}, u32[]{:S(2)}) async-start(bf16[8,8,4096]{2,1,0:T(8,128)(2,1)} %get-tuple-element.12), calls=%async_computation | async-start | bytes 1048576 | tf_op jit(solution)/shard_map/all_to_all | solution.py:356
  23.8 2.0 %collective-permute-start.3 = (bf16[64,4096]{1,0:T(8,128)(2,1)S(1)}, bf16[64,4096]{1,0:T(8,128)(2,1)S(1)}, u32[]{:S(2)}, u32[]{:S(2)}) collective-permute-start(bf16[64,4096]{1,0:T(8,128)(2,1)S(1)} %get-tuple-element.17), channel_id=1, source_target_pairs={{0,1},{1,0},{2,3},{3,2},{4,5},{5,4},{6,7},{7,6},{8,9},{9,8},{10,11... | collective-permute-start | bytes 1572872 | tf_op jit(solution)/shard_map/ppermute | solution.py:361
  26.7 25.7 %all-to-all-start.1 = ((bf16[8,8,4096]{2,1,0:T(8,128)(2,1)}), bf16[8,8,4096]{2,1,0:T(8,128)(2,1)S(1)}, u32[]{:S(2)}, u32[]{:S(2)}) async-start(bf16[8,8,4096]{2,1,0:T(8,128)(2,1)} %bitcast.2), calls=%async_computation.1 | async-start | bytes 1048576 | tf_op jit(solution)/shard_map/all_to_all | solution.py:363
  32.7 1.9 %collective-permute-start.2 = (bf16[64,4096]{1,0:T(8,128)(2,1)S(1)}, bf16[64,4096]{1,0:T(8,128)(2,1)S(1)}, u32[]{:S(2)}, u32[]{:S(2)}) collective-permute-start(bf16[64,4096]{1,0:T(8,128)(2,1)S(1)} %bitcast.3), channel_id=1, source_target_pairs={{0,1},{1,0},{2,3},{3,2},{4,5},{5,4},{6,7},{7,6},{8,9},{9,8},{10,11... | collective-permute-start | bytes 1572872 | tf_op jit(solution)/shard_map/ppermute | solution.py:358
